TPU v7x, 32 devices: a whole 2x2x4 slice. The times are simulated.
32 devices in a mesh: shard: 2 (over x), ctx: 4 (over z), tp: 4 (over y, core).
Axes of the slice: x: 2, y: 2, z: 4, core: 2. Of those that a mesh axis runs over, the one named last changes fastest.
Arguments:
- hidden_in: bfloat16 [8, 1024, 768], P('shard', 'ctx'), may hold values from -6 to 6
- token_type: int32 [8, 1024], P('shard', 'ctx'), may hold values 0 or 1
- segment: int32 [8, 1024], P('shard', 'ctx'), may hold values from 0 to 17, as said below
- query_weight: bfloat16 [4, 768, 768], P(None, 'shard', 'tp'), may hold values from -0.21875 to 0.21875
- key_value_weight: bfloat16 [2, 768, 768], P(None, 'shard', 'tp'), may hold values from -0.21875 to 0.21875
- query_bias: float32 [4, 768], P(None, 'tp'), may hold values from -1.75 to 1.75
- value_bias: float32 [768], P('tp'), may hold values from -1.75 to 1.75
- out_weight: bfloat16 [768, 768], P('tp', 'shard'), may hold values from -1.75 to 1.75
- out_bias: float32 [768], replicated, may hold values from -1.75 to 1.75
- norm1_gain: float32 [768], replicated, may hold values from 0.5 to 1.5
- norm1_bias: float32 [768], replicated, may hold values from -1.75 to 1.75
- up_weight: bfloat16 [768, 3072], P('shard', 'tp'), may hold values from -0.21875 to 0.21875
- up_bias: float32 [3072], P('tp'), may hold values from -1.75 to 1.75
- down_weight: bfloat16 [3072, 768], P('tp', 'shard'), may hold values from -0.109375 to 0.109375
- down_bias: float32 [768], replicated, may hold values from -1.75 to 1.75
- norm2_gain: float32 [768], replicated, may hold values from 0.5 to 1.5
- norm2_bias: float32 [768], replicated, may hold values from -1.75 to 1.75
- out_grad: bfloat16 [8, 1024, 768], P('shard', 'ctx'), may hold values from -6 to 6
Outputs:
- hidden_out: bfloat16 [8, 1024, 768], P('shard', 'ctx')
- in_grad: float32 [8, 1024, 768], P('shard', 'ctx')
- query_weight_grad: float32 [4, 768, 768], P(None, 'shard', 'tp')
- key_value_weight_grad: float32 [2, 768, 768], P(None, 'shard', 'tp')
- query_bias_grad: float32 [4, 768], P(None, 'tp')
- value_bias_grad: float32 [768], P('tp')
- out_weight_grad: float32 [768, 768], P('tp', 'shard')
- out_bias_grad: float32 [768], replicated
- norm1_gain_grad: float32 [768], replicated
- norm1_bias_grad: float32 [768], replicated
- up_weight_grad: float32 [768, 3072], P('shard', 'tp')
- up_bias_grad: float32 [3072], P('tp')
- down_weight_grad: float32 [3072, 768], P('tp', 'shard')
- down_bias_grad: float32 [768], replicated
- norm2_gain_grad: float32 [768], replicated
- norm2_bias_grad: float32 [768], replicated
Inputs may be any that keep to these rules, and one draw needn't show every extreme that they name: `token_type`: 0 marks a word, 1 an entity. `segment`: within each sequence the documents are numbered 1, 2, 3 in order, each holds 60 to 800 consecutive positions, and the positions after the last document are 0.
All inputs are finite; a program needn't handle non-finite values. No bound on the sum of `token_type` on one device may be relied on, other than what follows from the above.
Results may differ from a plain program's by a relative error of at most 0.02.
Values may be sent and summed in bfloat16 or wider, within the bound.
A program may use at most 128 MiB of HBM per device.

v0:
```python
import jax
import jax.numpy as jnp
from jax import lax
from jax.sharding import PartitionSpec as P

HEAD = 64
FF = 3072
eps_norm = 1e-05
big_neg = -1e30
root_half = 0.7071067811865476
inv_root_two_pi = 0.3989422804014327


def norm_forward(values, gain_vec, bias_vec):
    average = jnp.mean(values, axis=-1, keepdims=True)
    centred = values - average
    variance = jnp.mean(centred * centred, axis=-1, keepdims=True)
    inv_spread = lax.rsqrt(variance + eps_norm)
    normed = centred * inv_spread
    return (normed * gain_vec + bias_vec, normed, inv_spread)


def norm_backward(upstream, normed, inv_spread, gain_vec):
    scaled = upstream * gain_vec
    mean_first = jnp.mean(scaled, axis=-1, keepdims=True)
    second = jnp.mean(scaled * normed, axis=-1, keepdims=True)
    return inv_spread * (scaled - mean_first - normed * second)


def head_scores(queries, key_block, key_word):
    toward_word = jnp.einsum(
        "sqc,skc->sqk", queries[0], key_block, preferred_element_type=jnp.float32
    )
    toward_entity = jnp.einsum(
        "sqc,skc->sqk", queries[1], key_block, preferred_element_type=jnp.float32
    )
    return jnp.where(key_word, toward_word, toward_entity) * HEAD ** (-0.5)


def widen_cols(vector, full_width, offset):
    blank = jnp.zeros(vector.shape[:-1] + (full_width,), jnp.float32)
    return lax.dynamic_update_slice_in_dim(blank, vector, offset, vector.ndim - 1)


def per_device(
    hidden_in,
    token_type,
    segment,
    query_weight,
    key_value_weight,
    query_bias,
    value_bias,
    out_weight,
    out_bias,
    norm1_gain,
    norm1_bias,
    up_weight,
    up_bias,
    down_weight,
    down_bias,
    norm2_gain,
    norm2_bias,
    out_grad,
):
    seq_count, local_len, model_width = hidden_in.shape
    row_count = seq_count * local_len
    tensor_count = lax.axis_size("tp")
    tensor_rank = lax.axis_index("tp")
    share_rows = row_count // tensor_count
    share_start = tensor_rank * share_rows

    def own_rows(values):
        return lax.dynamic_slice_in_dim(values, share_start, share_rows, 0)

    weights_query, weights_keyval, weights_out, weights_up, weights_down = (
        lax.all_gather(query_weight, "shard", axis=1, tiled=True),
        lax.all_gather(key_value_weight, "shard", axis=1, tiled=True),
        lax.all_gather(out_weight, "shard", axis=1, tiled=True),
        lax.all_gather(up_weight, "shard", axis=0, tiled=True),
        lax.all_gather(down_weight, "shard", axis=1, tiled=True),
    )
    part_width = weights_query.shape[2]
    feed_width = weights_up.shape[1]
    heads_here = part_width // HEAD
    row_data = hidden_in.reshape(row_count, model_width)
    is_word = (token_type.reshape(row_count) == 0)[:, None]
    query_four = (
        jnp.einsum("rd,kde->kre", row_data, weights_query, preferred_element_type=jnp.float32)
        + query_bias[:, None, :]
    )
    chosen = jnp.stack(
        [
            jnp.where(is_word, query_four[0], query_four[2]),
            jnp.where(is_word, query_four[1], query_four[3]),
        ]
    ).astype(jnp.bfloat16)
    key_values = jnp.einsum(
        "rd,kde->kre", row_data, weights_keyval, preferred_element_type=jnp.float32
    )
    key_values = (
        key_values + jnp.stack([jnp.zeros_like(value_bias), value_bias])[:, None, :]
    ).astype(jnp.bfloat16)

    def by_head(values):
        return values.reshape(2, seq_count, local_len, heads_here, HEAD).transpose(3, 0, 1, 2, 4)

    def by_rows(values):
        return values.transpose(1, 2, 3, 0, 4).reshape(2, row_count, part_width)

    query_heads = by_head(chosen)
    keys_all = lax.all_gather(by_head(key_values), "ctx", axis=3, tiled=True)
    types_all, segments_all = (
        lax.all_gather(token_type, "ctx", axis=1, tiled=True),
        lax.all_gather(segment, "ctx", axis=1, tiled=True),
    )
    key_word = (types_all == 0)[:, None, :]
    allowed = (segment[:, :, None] == segments_all[:, None, :]) & (segments_all[:, None, :] > 0)

    def attend_head(pieces):
        queries, key_value = pieces
        scores = head_scores(queries, key_value[0], key_word)
        row_max = jnp.max(jnp.where(allowed, scores, big_neg), axis=-1, keepdims=True)
        exponent = jnp.exp(jnp.where(allowed, scores - row_max, big_neg))
        denominator = jnp.maximum(jnp.sum(exponent, axis=-1, keepdims=True), 1.0)
        probability = (exponent / denominator).astype(jnp.bfloat16)
        context = jnp.einsum(
            "sqk,skc->sqc", probability, key_value[1], preferred_element_type=jnp.float32
        )
        return (context.astype(jnp.bfloat16), row_max, denominator)

    context_heads, row_maxima, denominators = lax.map(attend_head, (query_heads, keys_all))
    context = context_heads.transpose(1, 2, 0, 3).reshape(row_count, part_width)
    attn_terms = jnp.dot(context, weights_out, preferred_element_type=jnp.float32)
    grad_output = out_grad.reshape(row_count, model_width).astype(jnp.float32)
    attention = lax.psum(attn_terms.astype(jnp.bfloat16), "tp").astype(jnp.float32) + out_bias
    first_out, first_hat, first_inv = norm_forward(
        row_data.astype(jnp.float32) + attention, norm1_gain, norm1_bias
    )
    first_low = first_out.astype(jnp.bfloat16)
    up_value = jnp.dot(first_low, weights_up, preferred_element_type=jnp.float32) + up_bias
    normal_cdf = 0.5 * (1.0 + lax.erf(up_value * root_half))
    active = jax.nn.gelu(up_value, approximate=False).astype(jnp.bfloat16)
    up_value, normal_cdf, active, down_terms = (
        up_value,
        normal_cdf,
        active,
        jnp.dot(active, weights_down, preferred_element_type=jnp.float32),
    )
    feed_out = lax.psum(down_terms.astype(jnp.bfloat16), "tp").astype(jnp.float32) + down_bias
    final_out, second_hat, second_inv = norm_forward(first_out + feed_out, norm2_gain, norm2_bias)
    hidden_out = final_out.astype(jnp.bfloat16).reshape(seq_count, local_len, model_width)
    grad_second = norm_backward(grad_output, second_hat, second_inv, norm2_gain)
    grad_feed = grad_second.astype(jnp.bfloat16)
    grad_down = jnp.dot(active.T, grad_feed, preferred_element_type=jnp.float32)
    grad_active = jnp.dot(grad_feed, weights_down.T, preferred_element_type=jnp.float32)
    gelu_slope = normal_cdf + up_value * jnp.exp(-0.5 * up_value * up_value) * inv_root_two_pi
    grad_up = (grad_active * gelu_slope).astype(jnp.bfloat16)
    grad_upw = jnp.dot(first_low.T, grad_up, preferred_element_type=jnp.float32)
    up_terms = jnp.dot(grad_up, weights_up.T, preferred_element_type=jnp.float32)
    grad_down, grad_up, grad_upw, up_terms = (grad_down, grad_up, grad_upw, up_terms)
    grad_first = grad_second + lax.psum(up_terms.astype(jnp.bfloat16), "tp").astype(jnp.float32)
    grad_first_in = norm_backward(grad_first, first_hat, first_inv, norm1_gain)
    grad_attention = grad_first_in.astype(jnp.bfloat16)
    first_hat_own, grad_first_own = (own_rows(first_hat), own_rows(grad_first))
    second_hat_own, grad_output_own = (own_rows(second_hat), own_rows(grad_output))
    grad_attn_own, grad_feed_own = (own_rows(grad_attention), own_rows(grad_feed))
    grad_outw = jnp.dot(context.T, grad_attention, preferred_element_type=jnp.float32)
    grad_context = jnp.dot(
        grad_attention, weights_out.T, preferred_element_type=jnp.float32
    ).astype(jnp.bfloat16)
    grad_context_heads = grad_context.reshape(seq_count, local_len, heads_here, HEAD).transpose(
        2, 0, 1, 3
    )

    def attend_back(pieces):
        queries, key_value, grad_ctx_head, row_max, denominator = pieces
        scores = head_scores(queries, key_value[0], key_word)
        probability = jnp.exp(jnp.where(allowed, scores - row_max, big_neg)) / denominator
        grad_weights = jnp.einsum(
            "sqc,skc->sqk", grad_ctx_head, key_value[1], preferred_element_type=jnp.float32
        )
        row_dot = jnp.sum(probability * grad_weights, axis=-1, keepdims=True)
        grad_scores = (probability * (grad_weights - row_dot)).astype(jnp.bfloat16) * jnp.bfloat16(
            HEAD ** (-0.5)
        )
        zero_block = jnp.zeros_like(grad_scores)
        grad_word = jnp.where(key_word, grad_scores, zero_block)
        grad_entity = jnp.where(key_word, zero_block, grad_scores)
        grad_queries = jnp.stack(
            [
                jnp.einsum(
                    "sqk,skc->sqc", grad_word, key_value[0], preferred_element_type=jnp.float32
                ),
                jnp.einsum(
                    "sqk,skc->sqc", grad_entity, key_value[0], preferred_element_type=jnp.float32
                ),
            ]
        )
        grad_keys = jnp.einsum(
            "sqk,sqc->skc", grad_word, queries[0], preferred_element_type=jnp.float32
        )
        grad_keys = grad_keys + jnp.einsum(
            "sqk,sqc->skc", grad_entity, queries[1], preferred_element_type=jnp.float32
        )
        grad_values = jnp.einsum(
            "sqk,sqc->skc",
            probability.astype(jnp.bfloat16),
            grad_ctx_head,
            preferred_element_type=jnp.float32,
        )
        return (grad_queries, jnp.stack([grad_keys, grad_values]))

    grad_query_heads, grad_kv_heads = lax.map(
        attend_back, (query_heads, keys_all, grad_context_heads, row_maxima, denominators)
    )
    grad_kv_mine = lax.psum_scatter(
        grad_kv_heads.astype(jnp.bfloat16), "ctx", scatter_dimension=3, tiled=True
    ).astype(jnp.float32)
    grad_keyval = by_rows(grad_kv_mine).astype(jnp.bfloat16)
    grad_chosen = by_rows(grad_query_heads).astype(jnp.bfloat16)
    zero_rows = jnp.zeros_like(grad_chosen[0])
    grad_query_four = jnp.stack(
        [
            jnp.where(is_word, grad_chosen[0], zero_rows),
            jnp.where(is_word, grad_chosen[1], zero_rows),
            jnp.where(is_word, zero_rows, grad_chosen[0]),
            jnp.where(is_word, zero_rows, grad_chosen[1]),
        ]
    )
    grad_queryw = jnp.einsum(
        "rd,kre->kde", row_data, grad_query_four, preferred_element_type=jnp.float32
    )
    grad_keyvalw = jnp.einsum(
        "rd,kre->kde", row_data, grad_keyval, preferred_element_type=jnp.float32
    )
    back_input = jnp.einsum(
        "kre,kde->rd", grad_query_four, weights_query, preferred_element_type=jnp.float32
    )
    back_input = back_input + jnp.einsum(
        "kre,kde->rd", grad_keyval, weights_keyval, preferred_element_type=jnp.float32
    )
    in_grad = (
        grad_first_in + lax.psum(back_input.astype(jnp.bfloat16), "tp").astype(jnp.float32)
    ).reshape(seq_count, local_len, model_width)
    column_at = tensor_rank * part_width
    feed_at = tensor_rank * feed_width
    small_grads = lax.psum(
        (
            jnp.sum(grad_first_own * first_hat_own, axis=0),
            jnp.sum(grad_first_own, axis=0),
            jnp.sum(grad_output_own * second_hat_own, axis=0),
            jnp.sum(grad_output_own, axis=0),
            jnp.sum(grad_attn_own, axis=0, dtype=jnp.float32),
            jnp.sum(grad_feed_own, axis=0, dtype=jnp.float32),
            widen_cols(jnp.sum(grad_query_four, axis=1, dtype=jnp.float32), model_width, column_at),
            widen_cols(jnp.sum(grad_keyval[1], axis=0, dtype=jnp.float32), model_width, column_at),
            widen_cols(jnp.sum(grad_up, axis=0, dtype=jnp.float32), FF, feed_at),
        ),
        ("shard", "ctx", "tp"),
    )
    (
        gain_one_grad,
        shift_one_grad,
        gain_two_grad,
        shift_two_grad,
        out_shift_grad,
        down_shift_grad,
        query_full,
        value_full,
        up_full,
    ) = small_grads
    query_shift_grad = lax.dynamic_slice_in_dim(query_full, column_at, part_width, 1)
    value_shift_grad = lax.dynamic_slice_in_dim(value_full, column_at, part_width, 0)
    up_shift_grad = lax.dynamic_slice_in_dim(up_full, feed_at, feed_width, 0)
    weight_grads = (grad_queryw, grad_keyvalw, grad_outw, grad_upw, grad_down)
    summed = (
        lax.psum(weight_grads[0].astype(jnp.bfloat16), "ctx").astype(jnp.float32),
        lax.psum(weight_grads[1].astype(jnp.bfloat16), "ctx").astype(jnp.float32),
        lax.psum(weight_grads[2].astype(jnp.bfloat16), "ctx").astype(jnp.float32),
        lax.psum(weight_grads[3].astype(jnp.bfloat16), "ctx").astype(jnp.float32),
        lax.psum(weight_grads[4].astype(jnp.bfloat16), "ctx").astype(jnp.float32),
    )
    my_grads = (
        lax.psum_scatter(
            summed[0].astype(jnp.bfloat16), "shard", scatter_dimension=1, tiled=True
        ).astype(jnp.float32),
        lax.psum_scatter(
            summed[1].astype(jnp.bfloat16), "shard", scatter_dimension=1, tiled=True
        ).astype(jnp.float32),
        lax.psum_scatter(
            summed[2].astype(jnp.bfloat16), "shard", scatter_dimension=1, tiled=True
        ).astype(jnp.float32),
        lax.psum_scatter(
            summed[3].astype(jnp.bfloat16), "shard", scatter_dimension=0, tiled=True
        ).astype(jnp.float32),
        lax.psum_scatter(
            summed[4].astype(jnp.bfloat16), "shard", scatter_dimension=1, tiled=True
        ).astype(jnp.float32),
    )
    return (
        hidden_out,
        in_grad,
        my_grads[0],
        my_grads[1],
        query_shift_grad,
        value_shift_grad,
        my_grads[2],
        out_shift_grad,
        gain_one_grad,
        shift_one_grad,
        my_grads[3],
        up_shift_grad,
        my_grads[4],
        down_shift_grad,
        gain_two_grad,
        shift_two_grad,
    )


def solution(mesh):
    in_specs = (
        P("shard", "ctx", None),
        P("shard", "ctx"),
        P("shard", "ctx"),
        P(None, "shard", "tp"),
        P(None, "shard", "tp"),
        P(None, "tp"),
        P("tp"),
        P("tp", "shard"),
        P(),
        P(),
        P(),
        P("shard", "tp"),
        P("tp"),
        P("tp", "shard"),
        P(),
        P(),
        P(),
        P("shard", "ctx", None),
    )
    out_specs = (
        P("shard", "ctx", None),
        P("shard", "ctx", None),
        P(None, "shard", "tp"),
        P(None, "shard", "tp"),
        P(None, "tp"),
        P("tp"),
        P("tp", "shard"),
        P(),
        P(),
        P(),
        P("shard", "tp"),
        P("tp"),
        P("tp", "shard"),
        P(),
        P(),
        P(),
    )
    return jax.shard_map(
        per_device, mesh=mesh, in_specs=in_specs, out_specs=out_specs, check_vma=False
    )
```

profile of v0, /device:TPU:0, one launch (start us, length us, event | category | flops | bytes accessed | tf_op | source)
XLA Modules:
  0.0 815.5 jit_solution(1495779303078105990)
XLA Ops:
  8.6 10.9 %all_gather.26 = bf16[2,768,192]{1,2,0:T(8,128)(2,1)S(1)} all-gather(bf16[2,384,192]{1,2,0:T(8,128)(2,1)} %param.26), channel_id=1, replica_groups=mesh['shard'=2,'ctx'=4,'tp'=4] {'shard'}, dimensions={1}, use_global_device_ids=true | all-gather | bytes 884736 | tf_op jit(solution)/shard_map/all_gather | solution.py:77
  24.4 13.6 %all_gather.24 = s32[4,1024]{1,0:T(4,128)S(1)} all-gather(s32[4,256]{1,0:T(4,128)S(1)} %copy-done.43), channel_id=1, replica_groups=mesh['shard'=2,'ctx'=4,'tp'=4] {'ctx'}, dimensions={1}, use_global_device_ids=true | all-gather | bytes 20480 | tf_op jit(solution)/shard_map/all_gather | solution.py:113
  38.1 13.3 %all_gather.28 = s32[4,1024]{1,0:T(4,128)S(1)} all-gather(s32[4,256]{1,0:T(4,128)S(1)} %copy-done.22), channel_id=1, replica_groups=mesh['shard'=2,'ctx'=4,'tp'=4] {'ctx'}, dimensions={1}, use_global_device_ids=true | all-gather | bytes 20480 | tf_op jit(solution)/shard_map/all_gather | solution.py:114
  51.3 5.9 all_gather.29
  58.4 2.7 add_bitcast_fusion
  64.9 35.8 %all-gather.7.cloned.1.call-done = bf16[3,2,4,1024,64]{3,4,2,1,0:T(8,128)(2,1)} async-done(((bf16[3,2,4,256,64]{3,4,2,1,0:T(8,128)(2,1)}), bf16[3,2,4,1024,64]{3,4,2,1,0:T(8,128)(2,1)}) %all-gather.7.cloned.1.call-update) | async-done | bytes 3145744 | tf_op jit(solution)/shard_map/all_gather | solution.py:111
  100.7 30.9 %while.28 = (s32[]{:T(128)}, bf16[3,4,256,64]{2,3,1,0:T(8,128)(2,1)}, f32[3,4,256,1]{2,1,3,0:T(4,128)}, f32[3,4,256,1]{2,1,3,0:T(4,128)}, pred[4,1,1024]{2,0,1:T...) while((s32[]{:T(128)}, ...), condition=%wide.region_3.4_spmd.clone, body=%wide.region_0.3_spmd.clone.sunk | while | flops 420544512 | bytes 23113960 | solution.py:131
  102.5 2.8 select_reduce_fusion.2
  107.1 3.3 fusion.170
  112.8 2.8 select_reduce_fusion.2
  117.4 3.3 fusion.170
  123.1 2.8 select_reduce_fusion.2
  127.7 3.3 fusion.170
  136.4 39.8 %all-reduce.9.cloned.1.call-done = bf16[1024,768]{1,0:T(8,128)(2,1)} async-done(((bf16[1024,768]{1,0:T(8,128)(2,1)}), bf16[1024,768]{1,0:T(8,128)(2,1)}) %all-reduce.9.cloned.1.call-update) | async-done | bytes 1572880 | tf_op jit(solution)/shard_map/psum | solution.py:135
  181.4 19.1 %all-gather.9.cloned.1.call-done = bf16[768,768]{1,0:T(8,128)(2,1)} async-done(((bf16[384,768]{1,0:T(8,128)(2,1)}), bf16[768,768]{1,0:T(8,128)(2,1)}) %all-gather.9.cloned.1.call-update) | async-done | bytes 1179664 | tf_op jit(solution)/shard_map/all_gather | solution.py:79
  200.5 10.3 %fusion.93 = (bf16[1024,768]{1,0:T(8,128)(2,1)}, f32[1024,768]{1,0:T(8,128)}) fusion(f32[768]{0:T(1024)S(1)} %copy-done.50, bf16[768,768]{1,0:T(8,128)(2,1)} %all-gather.9.cloned.1.call-done, f32[1024,768]{1,0:T(8,128)S(1)} %subtract_multiply_fusion.3, f32[768]{0:T(1024)S(1)} %copy-done.36, f32[768]{0:T(1024)S(1)} %copy-done.29), kind=kOutput, calls=%fused_computation.90 | convolution fusion | flops 1262223360 | bytes 9053184 | tf_op jit(solution)/shard_map/dot_general | solution.py:140
  210.7 13.9 %all-gather.11.cloned.1.call-done = bf16[768,768]{1,0:T(8,128)(2,1)} async-done(((bf16[768,384]{1,0:T(8,128)(2,1)}), bf16[768,768]{1,0:T(8,128)(2,1)}) %all-gather.11.cloned.1.call-update) | async-done | bytes 1179664 | tf_op jit(solution)/shard_map/all_gather | solution.py:80
  224.6 4.3 convolution_convert_fusion.1
  230.8 41.1 %all-reduce.11.cloned.1.call-done = bf16[1024,768]{1,0:T(8,128)(2,1)} async-done(((bf16[1024,768]{1,0:T(8,128)(2,1)}), bf16[1024,768]{1,0:T(8,128)(2,1)}) %all-reduce.11.cloned.1.call-update) | async-done | bytes 1572880 | tf_op jit(solution)/shard_map/psum | solution.py:149
  281.3 3.4 convert_reduce_fusion
  288.7 42.8 %all-reduce.13.cloned.1.call-done = bf16[1024,768]{1,0:T(8,128)(2,1)} async-done(((bf16[1024,768]{1,0:T(8,128)(2,1)}), bf16[1024,768]{1,0:T(8,128)(2,1)}) %all-reduce.13.cloned.1.call-update) | async-done | bytes 1572880 | tf_op jit(solution)/shard_map/psum | solution.py:161
  331.5 4.8 multiply_reduce_fusion.6
  343.8 150.3 %while.29 = (s32[]{:T(128)}, bf16[3,2,4,256,64]{3,4,2,1,0:T(8,128)(2,1)}, bf16[3,2,4,1024,64]{3,4,2,1,0:T(8,128)(2,1)}, pred[4,1,1024]{2,0,1:T(4,128)(4,1)}, bf1...) while((s32[]{:T(128)}, ...), condition=%wide.region_17.18_spmd.clone, body=%wide.region_15.17_spmd.clone.sunk | while | flops 1123033088 | bytes 97640736 | solution.py:213
  344.5 3.8 fusion.179
  350.1 5.1 exponential_divide_fusion.2
  355.2 7.7 fusion.181
  362.9 7.7 fusion.180
  372.3 3.5 fusion.183
  375.8 7.9 fusion.184
  383.7 8.0 fusion.185
  394.6 3.8 fusion.179
  400.2 5.0 exponential_divide_fusion.2
  405.3 7.7 fusion.181
  413.0 7.7 fusion.180
  422.4 3.5 fusion.183
  425.9 7.9 fusion.184
  433.8 8.0 fusion.185
  444.7 3.8 fusion.179
  450.3 5.0 exponential_divide_fusion.2
  455.4 7.7 fusion.181
  463.1 7.7 fusion.180
  472.5 3.5 fusion.183
  476.0 7.9 fusion.184
  483.8 8.0 fusion.185
  500.0 4.6 convolution_convert_fusion.3
  514.9 3.8 fusion.110
  518.7 3.6 copy.56
  522.3 4.0 reshape.227
  526.4 28.3 %reduce-scatter.15.cloned.1.call-done = bf16[3,2,4,256,64]{3,4,2,1,0:T(8,128)(2,1)} async-done(((bf16[3,2,4,1024,64]{3,4,2,1,0:T(8,128)(2,1)}), bf16[3,2,4,256,64]{3,4,2,1,0:T(8,128)(2,1)}) %reduce-scatter.15.cloned.1.call-update) | async-done | bytes 786448 | tf_op jit(solution)/shard_map/reduce_scatter | solution.py:216
  554.7 2.6 copy.55
  559.9 3.3 fusion.112
  563.1 3.0 copy.58
  566.1 3.0 reshape.229
  569.2 3.9 convolution_convert_fusion.4
  573.4 3.2 fusion.120
  580.6 14.0 %reduce-scatter.25.cloned.1.call-done = bf16[384,768]{1,0:T(8,128)(2,1)} async-done(((bf16[768,768]{1,0:T(8,128)(2,1)}), bf16[384,768]{1,0:T(8,128)(2,1)}) %reduce-scatter.25.cloned.1.call-update) | async-done | bytes 589840
  596.7 22.6 %reduce-scatter.19.cloned.1.call-done = bf16[384,768]{1,0:T(8,128)(2,1)} async-done(((bf16[768,768]{1,0:T(8,128)(2,1)}), bf16[384,768]{1,0:T(8,128)(2,1)}) %reduce-scatter.19.cloned.1.call-update) | async-done | bytes 589840
  619.3 2.9 reshape.228
  624.3 12.5 %reduce-scatter.21.cloned.1.call-done = bf16[384,384]{1,0:T(8,128)(2,1)} async-done(((bf16[768,384]{1,0:T(8,128)(2,1)}), bf16[384,384]{1,0:T(8,128)(2,1)}) %reduce-scatter.21.cloned.1.call-update) | async-done | bytes 294928
  639.3 22.2 %reduce-scatter.17.cloned.1.call-done = bf16[384,768]{1,0:T(8,128)(2,1)} async-done(((bf16[768,768]{1,0:T(8,128)(2,1)}), bf16[384,768]{1,0:T(8,128)(2,1)}) %reduce-scatter.17.cloned.1.call-update) | async-done | bytes 589840 | tf_op jit(solution)/shard_map/reduce_scatter | solution.py:293
  661.5 3.4 bitcast_convert_fusion
  675.8 41.3 %all-reduce.1 = (f32[4,768]{1,0:T(4,128)S(1)}, f32[768]{0:T(1024)S(1)}, f32[768]{0:T(1024)}, f32[768]{0:T(1024)}, f32[768]{0:T(1024)}, /*index=5*/f32[3072]{0:T(...) all-reduce(f32[4,768]{1,0:T(4,128)S(1)} %dynamic_update_slice.28, ...), channel_id=1, replica_groups=mesh['shard'=2,'ctx'=4,'tp'=4] {'shard','ctx','tp'}, use_global_device_ids=true, to_apply=%region_25.26 | all-reduce | flops 11520 | bytes 92160 | tf_op jit(solution)/shard_map/psum | solution.py:247
  719.1 4.1 convert_add_fusion
  723.2 77.6 %all-reduce.17.cloned.1.call-done = (bf16[4,384,192]{1,2,0:T(8,128)(2,1)}, bf16[2,384,192]{1,2,0:T(8,128)(2,1)}, bf16[192,384]{1,0:T(8,128)(2,1)}, bf16[384,768]{1,0:T(8,128)(2,1)}, bf16[768,384]{1,0:T(8,128)(2,1)}) async-done(((bf16[4,384,192]{1,2,0:T(8,128)(2,1)}, bf16[2,384,192]{1,2,0:T(8,128)(2,1)}, bf16[192,384]{1,0:T(8,128)(2,1)}, bf16[384,768]{1,0:T(8,128)(2,1)}, bf16[768,384]{1,0:T(8,128)(2,1)}), ...) | async-done | bytes 2211856 | tf_op jit(solution)/shard_map/psum | solution.py:277
  (266 shorter events, 126.1 us)
Async XLA Ops:
  7.2 51.2 %all-gather.5.cloned.1.call-start = ((), (), s32[]{:S(2)}) async-start(), calls=%async_computation.6 | async-start | bytes 1769472 | tf_op jit(solution)/shard_map/all_gather | solution.py:76
  7.9 92.7 %all-gather.7.cloned.1.call-start = ((), (), s32[]{:S(2)}) async-start(), calls=%async_computation.7 | async-start | bytes 3932160 | tf_op jit(solution)/shard_map/all_gather | solution.py:111
  20.4 4.0 copy-start.43
  20.4 17.7 %copy-start.22 = (s32[4,256]{1,0:T(4,128)S(1)}, s32[4,256]{1,0:T(4,128)}, u32[]{:S(2)}) copy-start(s32[4,256]{1,0:T(4,128)} %param.24) | copy-start | bytes 12292
  20.4 31.0 %copy-start.31 = (bf16[192,384]{1,0:T(8,128)(2,1)S(1)}, bf16[192,384]{1,0:T(8,128)(2,1)}, u32[]{:S(2)}) copy-start(bf16[192,384]{1,0:T(8,128)(2,1)} %param.29) | copy-start | bytes 442372
  22.6 35.8 %copy-start.3 = (bf16[4,256,768]{2,1,0:T(8,128)(2,1)S(1)}, bf16[4,256,768]{2,1,0:T(8,128)(2,1)}, u32[]{:S(2)}) copy-start(bf16[4,256,768]{2,1,0:T(8,128)(2,1)} %param.22) | copy-start | bytes 4718596
  22.7 35.8 %copy-start.49 = (f32[4,192]{1,0:T(4,128)S(1)}, f32[4,192]{1,0:T(4,128)}, u32[]{:S(2)}) copy-start(f32[4,192]{1,0:T(4,128)} %param.27) | copy-start | bytes 9220
  24.3 151.9 %all-reduce.9.cloned.1.call-start = ((), (), s32[]{:S(2)}) async-start(), calls=%async_computation.8 | async-start | bytes 3145728 | tf_op jit(solution)/shard_map/psum | solution.py:135
  24.4 36.7 %copy-start.44 = (pred[1024]{0:T(1024)(128)(4,1)}, pred[1024]{0:T(1024)(128)(4,1)S(1)}, u32[]{:S(2)}) copy-start(pred[1024]{0:T(1024)(128)(4,1)S(1)} %eq.36) | copy-start | bytes 3076
  100.7 32.6 %copy-start.19 = (bf16[192,768]{1,0:T(8,128)(2,1)S(1)}, bf16[192,768]{1,0:T(8,128)(2,1)}, u32[]{:S(2)}) copy-start(bf16[192,768]{1,0:T(8,128)(2,1)} %all_gather.29) | copy-start | bytes 884740
  100.7 1.8 copy-start.23
  100.7 1.9 copy-start.25
  100.7 1.9 copy-start.27
  111.0 1.9 copy-start.27
  121.3 1.8 copy-start.27
  131.5 4.7 copy-start.6
  131.5 44.7 %copy-start.42 = (f32[768]{0:T(1024)S(1)}, f32[768]{0:T(1024)}, u32[]{:S(2)}) copy-start(f32[768]{0:T(1024)} %param.30) | copy-start | bytes 9220
  133.2 45.1 %copy-start.8 = (bf16[24,8,4,256]{3,1,2,0:T(8,128)(2,1)}, bf16[24,8,4,256]{3,1,2,0:T(8,128)(2,1)S(1)}, u32[]{:S(2)}) copy-start(bf16[24,8,4,256]{3,1,2,0:T(8,128)(2,1)S(1)} %copy.64) | copy-start | bytes 1179652
  135.0 65.4 %all-gather.9.cloned.1.call-start = ((), (), s32[]{:S(2)}) async-start(), calls=%async_computation.9 | async-start | bytes 1769472 | tf_op jit(solution)/shard_map/all_gather | solution.py:79
  135.6 89.0 %all-gather.11.cloned.1.call-start = ((), (), s32[]{:S(2)}) async-start(), calls=%async_computation.10 | async-start | bytes 1769472 | tf_op jit(solution)/shard_map/all_gather | solution.py:80
  136.2 135.8 %all-reduce.11.cloned.1.call-start = ((), (), s32[]{:S(2)}) async-start(), calls=%async_computation.11 | async-start | bytes 3145728 | tf_op jit(solution)/shard_map/psum | solution.py:149
  176.2 2.1 copy-start.4
  179.3 157.1 %copy-start.33 = (f32[1024]{0:T(1024)}, f32[1024]{0:T(1024)S(1)}, u32[]{:S(2)}) copy-start(f32[1024]{0:T(1024)S(1)} %add_rsqrt_fusion.1) | copy-start | bytes 12292
  179.3 21.2 %copy-start.29 = (f32[768]{0:T(1024)S(1)}, f32[768]{0:T(1024)}, u32[]{:S(2)}) copy-start(f32[768]{0:T(1024)} %param.31) | copy-start | bytes 9220
  179.3 21.2 %copy-start.36 = (f32[768]{0:T(1024)S(1)}, f32[768]{0:T(1024)}, u32[]{:S(2)}) copy-start(f32[768]{0:T(1024)} %param.32) | copy-start | bytes 9220
  179.3 21.2 %copy-start.50 = (f32[768]{0:T(1024)S(1)}, f32[768]{0:T(1024)}, u32[]{:S(2)}) copy-start(f32[768]{0:T(1024)} %param.34) | copy-start | bytes 9220
  224.6 4.4 copy-start.32
  228.9 43.0 %copy-start.35 = (f32[768]{0:T(1024)S(1)}, f32[768]{0:T(1024)}, u32[]{:S(2)}) copy-start(f32[768]{0:T(1024)} %param.36) | copy-start | bytes 9220
  229.0 102.6 %all-reduce.13.cloned.1.call-start = ((), (), s32[]{:S(2)}) async-start(), calls=%async_computation.12 | async-start | bytes 3145728 | tf_op jit(solution)/shard_map/psum | solution.py:161
  272.0 2.2 copy-start.5
  277.3 2.2 copy-start.48
  277.3 3.9 copy-start.52
  279.0 5.6 copy-start.11
  281.3 4.6 copy-start.47
  285.9 45.7 %copy-start.46 = (f32[768]{0:T(1024)S(1)}, f32[768]{0:T(1024)}, u32[]{:S(2)}) copy-start(f32[768]{0:T(1024)} %param.38) | copy-start | bytes 9220
  288.5 266.2 %reduce-scatter.15.cloned.1.call-start = ((), (), s32[]{:S(2)}) async-start(), calls=%async_computation.13 | async-start | bytes 3932160 | tf_op jit(solution)/shard_map/reduce_scatter | solution.py:216
  348.2 1.9 copy-start.24
  348.2 1.9 copy-start.26
  348.2 1.9 copy-start.28
  398.3 1.9 copy-start.24
  398.3 1.9 copy-start.26
  398.3 1.9 copy-start.28
  448.4 1.9 copy-start.24
  448.4 1.9 copy-start.26
  448.4 1.9 copy-start.28
  494.1 84.8 %reduce-scatter.23.cloned.1.call-start = ((), (), s32[]{:S(2)}) async-start(), calls=%async_computation.18 | async-start | bytes 589824
  499.6 95.0 %reduce-scatter.25.cloned.1.call-start = ((), (), s32[]{:S(2)}) async-start(), calls=%async_computation.19 | async-start | bytes 1769472
  507.0 5.7 copy-start.45
  507.0 112.3 %reduce-scatter.19.cloned.1.call-start = ((), (), s32[]{:S(2)}) async-start(), calls=%async_computation.16 | async-start | bytes 1769472
  513.9 59.5 %copy-start.14 = (bf16[1,1024,192]{1,2,0:T(8,128)(2,1)}, bf16[1,1024,192]{1,2,0:T(8,128)(2,1)S(1)}, u32[]{:S(2)}) copy-start(bf16[1,1024,192]{1,2,0:T(8,128)(2,1)S(1)} %get-tuple-element.250) | copy-start | bytes 1179652
  526.3 110.5 %reduce-scatter.21.cloned.1.call-start = ((), (), s32[]{:S(2)}) async-start(), calls=%async_computation.17 | async-start | bytes 884736
  559.8 9.4 %copy-start.30 = (f32[768]{0:T(1024)S(1)}, f32[768]{0:T(1024)}, u32[]{:S(2)}) copy-start(f32[768]{0:T(1024)} %param.31) | copy-start | bytes 9220
  559.8 9.4 %copy-start.37 = (f32[768]{0:T(1024)S(1)}, f32[768]{0:T(1024)}, u32[]{:S(2)}) copy-start(f32[768]{0:T(1024)} %param.32) | copy-start | bytes 9220
  569.1 92.3 %reduce-scatter.17.cloned.1.call-start = ((), (), s32[]{:S(2)}) async-start(), calls=%async_computation.15 | async-start | bytes 1769472 | tf_op jit(solution)/shard_map/reduce_scatter | solution.py:293
  573.1 146.0 %all-reduce.15.cloned.1.call-start = ((), (), s32[]{:S(2)}) async-start(), calls=%async_computation.14 | async-start | bytes 3145728 | tf_op jit(solution)/shard_map/psum | solution.py:243
  573.4 3.2 copy-start.10
  573.4 3.2 copy-start.13
  578.8 222.0 %all-reduce.17.cloned.1.call-start = ((), (), s32[]{:S(2)}) async-start(), calls=%async_computation.20 | async-start | bytes 4423680 | tf_op jit(solution)/shard_map/psum | solution.py:277
  661.5 7.6 copy-start.15
  664.9 54.2 %copy-start.34 = (f32[1024]{0:T(1024)S(1)}, f32[1024]{0:T(1024)}, u32[]{:S(2)}) copy-start(f32[1024]{0:T(1024)} %copy-done.33) | copy-start | bytes 12292
  664.9 54.2 %copy-start.39 = (f32[1024]{0:T(1024)S(1)}, f32[1024]{0:T(1024)}, u32[]{:S(2)}) copy-start(f32[1024]{0:T(1024)} %copy-done.38) | copy-start | bytes 12292
  664.9 54.2 %copy-start.41 = (f32[1024]{0:T(1024)S(1)}, f32[1024]{0:T(1024)}, u32[]{:S(2)}) copy-start(f32[1024]{0:T(1024)} %copy-done.40) | copy-start | bytes 12292
  800.8 5.7 copy-start.21
  800.8 6.8 copy-start.20
  (16 other events, 22.4 us)
Sparse Core Ops, SparseCore 0:
  9.5 25.4 all-gather.4
  37.2 63.4 all-gather.6
  135.1 41.0 all-reduce.8
  177.6 22.7 all-gather.8
  201.8 22.7 all-gather.10
  229.1 42.8 all-reduce.10
  288.6 42.9 all-reduce.12
  494.2 60.4 reduce-scatter.14
  556.9 13.0 reduce-scatter.22
  572.7 21.8 reduce-scatter.24
  597.4 21.8 reduce-scatter.18
  621.4 15.3 reduce-scatter.20
  639.6 21.8 reduce-scatter.16
  663.7 43.4 all-reduce.14
  710.4 90.3 all-reduce.16
where the time goes:
time: 824 us; the launch traced here: 815 us
  waiting for transfers between devices  372 us (45%)
  matrix products  212 us (26%)
  blocking collectives  85 us (10%)
  local copies, waits for them, and re-layouts  66 us (8%)
  other arithmetic  64.1 us (8%)
  between operations  14.7 us (2%)
    psum x1, waiting for transfers between devices, per_device(): lax.psum(weight_grads[0].astype(jnp.bfloat16), 'ctx').astype(jnp.float32)  77.6 us
    unnamed x19, waiting for transfers between devices  51 us
    psum x1, waiting for transfers between devices, per_device(): lax.psum(up_terms.astype(jnp.bfloat16), 'tp').astype(jnp.float32)  42.8 us
    psum x1, blocking collectives, per_device(): lax.psum((jnp.sum(grad_first_own * first_hat_own, axis=0), jnp.sum(grad_f...  41.3 us
    psum x1, waiting for transfers between devices, per_device(): lax.psum(down_terms.astype(jnp.bfloat16), 'tp').astype(jnp.float32)  41.1 us
    psum x1, waiting for transfers between devices, per_device(): lax.psum(attn_terms.astype(jnp.bfloat16), 'tp').astype(jnp.float32)  39.8 us
    unnamed x108, local copies, waits for them, and re-layouts  38.4 us
    all_gather x1, waiting for transfers between devices, per_device(): keys_all = lax.all_gather(by_head(key_values), 'ctx', axis=3, tiled=True)  35.8 us
  transfers between devices with their start and end apart: 15, of which 12 were waited for; matrix products, arithmetic and copies ran while one was open for 14% of the time, Pallas kernels for 0%

commit v1 on v0

--- a/solution.py
+++ b/solution.py
@@ -273,8 +273,13 @@
     value_shift_grad = lax.dynamic_slice_in_dim(value_full, column_at, part_width, 0)
     up_shift_grad = lax.dynamic_slice_in_dim(up_full, feed_at, feed_width, 0)
     weight_grads = (grad_queryw, grad_keyvalw, grad_outw, grad_upw, grad_down)
+    take_ranges_over_axis = lambda vec, axis_key: jnp.sum(
+        lax.all_gather(vec, axis_name=axis_key), axis=0
+    )
     summed = (
-        lax.psum(weight_grads[0].astype(jnp.bfloat16), "ctx").astype(jnp.float32),
+        take_ranges_over_axis(weight_grads[0].astype(jnp.bfloat16), axis_key="ctx").astype(
+            jnp.float32
+        ),
         lax.psum(weight_grads[1].astype(jnp.bfloat16), "ctx").astype(jnp.float32),
         lax.psum(weight_grads[2].astype(jnp.bfloat16), "ctx").astype(jnp.float32),
         lax.psum(weight_grads[3].astype(jnp.bfloat16), "ctx").astype(jnp.float32),

time: 824 us -> 890 us (1.080)
  waiting for transfers between devices: 372 us -> 434 us
    all_gather x0 -> x1, waiting for transfers between devices: none -> 91.5 us  [per_device(): lax.all_gather(vec, axis_name=axis_key)]
    psum x1, waiting for transfers between devices: 77.6 us -> 43.7 us  [per_device(): lax.psum(weight_grads[1].astype(jnp.bfloat16), 'ctx').astype(jnp.float32)]
    reduce_scatter x1, waiting for transfers between devices: 28.3 us -> 47.6 us  [per_device(): lax.psum_scatter(grad_kv_heads.astype(jnp.bfloat16), 'ctx', scatter_dimen...]
    unnamed x19 -> x20, waiting for transfers between devices: 51 us -> 36.5 us
    unnamed x108 -> x106, local copies, waits for them, and re-layouts: 38.4 us -> 36.7 us
  transfers between devices with their start and end apart: 15 -> 16, of which waited for: 12 -> 13; matrix products, arithmetic and copies ran while one was open for 14% -> 14% of each run, Pallas kernels for 0% -> 0%
where the time goes in v1:
time: 890 us; the launch traced here: 881 us
  waiting for transfers between devices  434 us (49%)
  matrix products  212 us (24%)
  blocking collectives  86 us (10%)
  other arithmetic  68.5 us (8%)
  local copies, waits for them, and re-layouts  64.2 us (7%)
  between operations  14.7 us (2%)
    all_gather x1, waiting for transfers between devices, per_device(): lax.all_gather(vec, axis_name=axis_key)  91.5 us
    reduce_scatter x1, waiting for transfers between devices, per_device(): lax.psum_scatter(grad_kv_heads.astype(jnp.bfloat16), 'ctx', scatter_dimen...  47.6 us
    psum x1, waiting for transfers between devices, per_device(): lax.psum(weight_grads[1].astype(jnp.bfloat16), 'ctx').astype(jnp.float32)  43.7 us
    psum x1, waiting for transfers between devices, per_device(): lax.psum(up_terms.astype(jnp.bfloat16), 'tp').astype(jnp.float32)  42.8 us
    psum x1, blocking collectives, per_device(): lax.psum((jnp.sum(grad_first_own * first_hat_own, axis=0), jnp.sum(grad_f...  42.3 us
    psum x1, waiting for transfers between devices, per_device(): lax.psum(down_terms.astype(jnp.bfloat16), 'tp').astype(jnp.float32)  41.2 us
    psum x1, waiting for transfers between devices, per_device(): lax.psum(attn_terms.astype(jnp.bfloat16), 'tp').astype(jnp.float32)  39.8 us
    unnamed x106, local copies, waits for them, and re-layouts  36.7 us
  transfers between devices with their start and end apart: 16, of which 13 were waited for; matrix products, arithmetic and copies ran while one was open for 14% of the time, Pallas kernels for 0%

profile of v1, /device:TPU:0, one launch (start us, length us, event | category | flops | bytes accessed | tf_op | source)
XLA Modules:
  0.0 881.3 jit_solution(2027505078301370303)
XLA Ops:
  8.6 10.9 %all_gather.32 = bf16[2,768,192]{1,2,0:T(8,128)(2,1)S(1)} all-gather(bf16[2,384,192]{1,2,0:T(8,128)(2,1)} %param.26), channel_id=1, replica_groups=mesh['shard'=2,'ctx'=4,'tp'=4] {'shard'}, dimensions={1}, use_global_device_ids=true | all-gather | bytes 884736 | tf_op jit(solution)/shard_map/all_gather | solution.py:77
  24.4 13.6 %all_gather.30 = s32[4,1024]{1,0:T(4,128)S(1)} all-gather(s32[4,256]{1,0:T(4,128)S(1)} %copy-done.42), channel_id=1, replica_groups=mesh['shard'=2,'ctx'=4,'tp'=4] {'ctx'}, dimensions={1}, use_global_device_ids=true | all-gather | bytes 20480 | tf_op jit(solution)/shard_map/all_gather | solution.py:113
  38.1 13.3 %all_gather.34 = s32[4,1024]{1,0:T(4,128)S(1)} all-gather(s32[4,256]{1,0:T(4,128)S(1)} %copy-done.21), channel_id=1, replica_groups=mesh['shard'=2,'ctx'=4,'tp'=4] {'ctx'}, dimensions={1}, use_global_device_ids=true | all-gather | bytes 20480 | tf_op jit(solution)/shard_map/all_gather | solution.py:114
  51.3 5.9 all_gather.35
  58.4 2.7 add_bitcast_fusion
  64.9 35.8 %all-gather.9.cloned.1.call-done = bf16[3,2,4,1024,64]{3,4,2,1,0:T(8,128)(2,1)} async-done(((bf16[3,2,4,256,64]{3,4,2,1,0:T(8,128)(2,1)}), bf16[3,2,4,1024,64]{3,4,2,1,0:T(8,128)(2,1)}) %all-gather.9.cloned.1.call-update) | async-done | bytes 3145744 | tf_op jit(solution)/shard_map/all_gather | solution.py:111
  100.7 30.9 %while.28 = (s32[]{:T(128)}, bf16[3,4,256,64]{2,3,1,0:T(8,128)(2,1)}, f32[3,4,256,1]{2,1,3,0:T(4,128)}, f32[3,4,256,1]{2,1,3,0:T(4,128)}, pred[4,1,1024]{2,0,1:T...) while((s32[]{:T(128)}, ...), condition=%wide.region_3.4_spmd.clone, body=%wide.region_0.3_spmd.clone.sunk | while | flops 420544512 | bytes 23113960 | solution.py:131
  102.5 2.8 select_reduce_fusion.2
  107.1 3.3 fusion.170
  112.8 2.8 select_reduce_fusion.2
  117.4 3.3 fusion.170
  123.1 2.8 select_reduce_fusion.2
  127.7 3.3 fusion.170
  136.4 39.8 %all-reduce.9.cloned.1.call-done = bf16[1024,768]{1,0:T(8,128)(2,1)} async-done(((bf16[1024,768]{1,0:T(8,128)(2,1)}), bf16[1024,768]{1,0:T(8,128)(2,1)}) %all-reduce.9.cloned.1.call-update) | async-done | bytes 1572880 | tf_op jit(solution)/shard_map/psum | solution.py:135
  181.4 19.1 %all-gather.11.cloned.1.call-done = bf16[768,768]{1,0:T(8,128)(2,1)} async-done(((bf16[384,768]{1,0:T(8,128)(2,1)}), bf16[768,768]{1,0:T(8,128)(2,1)}) %all-gather.11.cloned.1.call-update) | async-done | bytes 1179664 | tf_op jit(solution)/shard_map/all_gather | solution.py:79
  200.5 10.3 %fusion.93 = (bf16[1024,768]{1,0:T(8,128)(2,1)}, f32[1024,768]{1,0:T(8,128)}) fusion(f32[768]{0:T(1024)S(1)} %copy-done.49, bf16[768,768]{1,0:T(8,128)(2,1)} %all-gather.11.cloned.1.call-done, f32[1024,768]{1,0:T(8,128)S(1)} %subtract_multiply_fusion.3, f32[768]{0:T(1024)S(1)} %copy-done.35, f32[768]{0:T(1024)S(1)} %copy-done.28), kind=kOutput, calls=%fused_computation.90 | convolution fusion | flops 1262223360 | bytes 9053184 | tf_op jit(solution)/shard_map/dot_general | solution.py:140
  210.8 13.9 %all-gather.13.cloned.1.call-done = bf16[768,768]{1,0:T(8,128)(2,1)} async-done(((bf16[768,384]{1,0:T(8,128)(2,1)}), bf16[768,768]{1,0:T(8,128)(2,1)}) %all-gather.13.cloned.1.call-update) | async-done | bytes 1179664 | tf_op jit(solution)/shard_map/all_gather | solution.py:80
  224.7 4.3 convolution_convert_fusion.1
  230.8 41.2 %all-reduce.11.cloned.1.call-done = bf16[1024,768]{1,0:T(8,128)(2,1)} async-done(((bf16[1024,768]{1,0:T(8,128)(2,1)}), bf16[1024,768]{1,0:T(8,128)(2,1)}) %all-reduce.11.cloned.1.call-update) | async-done | bytes 1572880 | tf_op jit(solution)/shard_map/psum | solution.py:149
  281.3 3.4 convert_reduce_fusion
  288.8 42.8 %all-reduce.13.cloned.1.call-done = bf16[1024,768]{1,0:T(8,128)(2,1)} async-done(((bf16[1024,768]{1,0:T(8,128)(2,1)}), bf16[1024,768]{1,0:T(8,128)(2,1)}) %all-reduce.13.cloned.1.call-update) | async-done | bytes 1572880 | tf_op jit(solution)/shard_map/psum | solution.py:161
  331.6 4.8 multiply_reduce_fusion.6
  343.8 150.2 %while.29 = (s32[]{:T(128)}, bf16[3,2,4,256,64]{3,4,2,1,0:T(8,128)(2,1)}, bf16[3,2,4,1024,64]{3,4,2,1,0:T(8,128)(2,1)}, pred[4,1,1024]{2,0,1:T(4,128)(4,1)}, bf1...) while((s32[]{:T(128)}, ...), condition=%wide.region_17.18_spmd.clone, body=%wide.region_15.17_spmd.clone.sunk | while | flops 1123033088 | bytes 97640736 | solution.py:213
  344.5 3.8 fusion.179
  350.1 5.0 exponential_divide_fusion.2
  355.2 7.7 fusion.181
  362.9 7.7 fusion.180
  372.3 3.5 fusion.183
  375.7 7.9 fusion.184
  383.6 8.0 fusion.185
  394.5 3.8 fusion.179
  400.2 5.0 exponential_divide_fusion.2
  405.2 7.7 fusion.181
  412.9 7.7 fusion.180
  422.3 3.5 fusion.183
  425.8 7.9 fusion.184
  433.7 8.0 fusion.185
  444.6 3.8 fusion.179
  450.2 5.0 exponential_divide_fusion.2
  455.3 7.7 fusion.181
  463.0 7.7 fusion.180
  472.4 3.5 fusion.183
  475.9 7.9 fusion.184
  483.7 8.0 fusion.185
  499.9 4.6 convolution_convert_fusion.3
  506.9 47.6 %reduce-scatter.15.cloned.1.call-done = bf16[3,2,4,256,64]{3,4,2,1,0:T(8,128)(2,1)} async-done(((bf16[3,2,4,1024,64]{3,4,2,1,0:T(8,128)(2,1)}), bf16[3,2,4,256,64]{3,4,2,1,0:T(8,128)(2,1)}) %reduce-scatter.15.cloned.1.call-update) | async-done | bytes 786448 | tf_op jit(solution)/shard_map/reduce_scatter | solution.py:216
  554.6 2.6 copy.55
  559.7 3.3 fusion.112
  563.0 3.0 copy.58
  566.0 3.0 reshape.230
  569.1 3.9 convolution_convert_fusion.4
  581.0 3.8 fusion.110
  584.9 3.2 fusion.120
  596.6 15.5 %reduce-scatter.21.cloned.1.call-done = bf16[384,384]{1,0:T(8,128)(2,1)} async-done(((bf16[768,384]{1,0:T(8,128)(2,1)}), bf16[384,384]{1,0:T(8,128)(2,1)}) %reduce-scatter.21.cloned.1.call-update) | async-done | bytes 294928
  614.6 22.1 %reduce-scatter.17.cloned.1.call-done = bf16[384,768]{1,0:T(8,128)(2,1)} async-done(((bf16[768,768]{1,0:T(8,128)(2,1)}), bf16[384,768]{1,0:T(8,128)(2,1)}) %reduce-scatter.17.cloned.1.call-update) | async-done | bytes 589840 | tf_op jit(solution)/shard_map/reduce_scatter | solution.py:298
  636.8 91.5 %all-gather.15.cloned.1.call-done = bf16[16,768,192]{1,2,0:T(8,128)(2,1)} async-done(((bf16[4,768,192]{1,2,0:T(8,128)(2,1)}), bf16[16,768,192]{1,2,0:T(8,128)(2,1)}) %all-gather.15.cloned.1.call-update) | async-done | bytes 4718608 | tf_op jit(solution)/shard_map/all_gather | solution.py:277
  728.3 4.4 reduce_sum.193
  732.6 3.6 copy.56
  736.3 4.0 reshape.228
  740.3 3.4 bitcast_convert_fusion
  754.6 42.3 %all-reduce.1 = (f32[4,768]{1,0:T(4,128)S(1)}, f32[768]{0:T(1024)S(1)}, f32[768]{0:T(1024)}, f32[768]{0:T(1024)}, f32[768]{0:T(1024)}, /*index=5*/f32[3072]{0:T(...) all-reduce(f32[4,768]{1,0:T(4,128)S(1)} %dynamic_update_slice.28, ...), channel_id=1, replica_groups=mesh['shard'=2,'ctx'=4,'tp'=4] {'shard','ctx','tp'}, use_global_device_ids=true, to_apply=%region_25.26 | all-reduce | flops 11520 | bytes 92160 | tf_op jit(solution)/shard_map/psum | solution.py:247
  798.9 4.1 convert_add_fusion
  803.0 43.7 %all-reduce.17.cloned.1.call-done = (bf16[2,384,192]{1,2,0:T(8,128)(2,1)}, bf16[192,384]{1,0:T(8,128)(2,1)}, bf16[384,768]{1,0:T(8,128)(2,1)}, bf16[768,384]{1,0:T(8,128)(2,1)}) async-done(((bf16[2,384,192]{1,2,0:T(8,128)(2,1)}, bf16[192,384]{1,0:T(8,128)(2,1)}, bf16[384,768]{1,0:T(8,128)(2,1)}, bf16[768,384]{1,0:T(8,128)(2,1)}), (bf16[2,384,192]{1,2,0:T(8,128)(2,1)}, bf16[192,384]{1,0:T(8,128)(2,1)}, ...) | async-done | bytes 1622032 | tf_op jit(solution)/shard_map/psum | solution.py:283
  853.5 16.8 %reduce-scatter.19.cloned.1.call-done = bf16[384,768]{1,0:T(8,128)(2,1)} async-done(((bf16[768,768]{1,0:T(8,128)(2,1)}), bf16[384,768]{1,0:T(8,128)(2,1)}) %reduce-scatter.19.cloned.1.call-update) | async-done | bytes 589840
  (268 shorter events, 129.5 us)
Async XLA Ops:
  7.2 51.2 %all-gather.7.cloned.1.call-start = ((), (), s32[]{:S(2)}) async-start(), calls=%async_computation.6 | async-start | bytes 1769472 | tf_op jit(solution)/shard_map/all_gather | solution.py:76
  7.9 92.7 %all-gather.9.cloned.1.call-start = ((), (), s32[]{:S(2)}) async-start(), calls=%async_computation.7 | async-start | bytes 3932160 | tf_op jit(solution)/shard_map/all_gather | solution.py:111
  20.4 4.0 copy-start.42
  20.4 17.7 %copy-start.21 = (s32[4,256]{1,0:T(4,128)S(1)}, s32[4,256]{1,0:T(4,128)}, u32[]{:S(2)}) copy-start(s32[4,256]{1,0:T(4,128)} %param.24) | copy-start | bytes 12292
  20.4 31.0 %copy-start.30 = (bf16[192,384]{1,0:T(8,128)(2,1)S(1)}, bf16[192,384]{1,0:T(8,128)(2,1)}, u32[]{:S(2)}) copy-start(bf16[192,384]{1,0:T(8,128)(2,1)} %param.29) | copy-start | bytes 442372
  22.6 35.8 %copy-start.3 = (bf16[4,256,768]{2,1,0:T(8,128)(2,1)S(1)}, bf16[4,256,768]{2,1,0:T(8,128)(2,1)}, u32[]{:S(2)}) copy-start(bf16[4,256,768]{2,1,0:T(8,128)(2,1)} %param.22) | copy-start | bytes 4718596
  22.7 35.8 %copy-start.48 = (f32[4,192]{1,0:T(4,128)S(1)}, f32[4,192]{1,0:T(4,128)}, u32[]{:S(2)}) copy-start(f32[4,192]{1,0:T(4,128)} %param.27) | copy-start | bytes 9220
  24.3 151.9 %all-reduce.9.cloned.1.call-start = ((), (), s32[]{:S(2)}) async-start(), calls=%async_computation.8 | async-start | bytes 3145728 | tf_op jit(solution)/shard_map/psum | solution.py:135
  24.4 36.7 %copy-start.43 = (pred[1024]{0:T(1024)(128)(4,1)}, pred[1024]{0:T(1024)(128)(4,1)S(1)}, u32[]{:S(2)}) copy-start(pred[1024]{0:T(1024)(128)(4,1)S(1)} %eq.36) | copy-start | bytes 3076
  100.7 32.6 %copy-start.19 = (bf16[192,768]{1,0:T(8,128)(2,1)S(1)}, bf16[192,768]{1,0:T(8,128)(2,1)}, u32[]{:S(2)}) copy-start(bf16[192,768]{1,0:T(8,128)(2,1)} %all_gather.35) | copy-start | bytes 884740
  100.7 1.9 copy-start.24
  100.7 1.9 copy-start.26
  111.0 1.8 copy-start.24
  111.0 1.9 copy-start.26
  121.3 1.8 copy-start.26
  131.6 4.7 copy-start.6
  131.6 44.7 %copy-start.41 = (f32[768]{0:T(1024)S(1)}, f32[768]{0:T(1024)}, u32[]{:S(2)}) copy-start(f32[768]{0:T(1024)} %param.30) | copy-start | bytes 9220
  133.2 45.1 %copy-start.8 = (bf16[24,8,4,256]{3,1,2,0:T(8,128)(2,1)}, bf16[24,8,4,256]{3,1,2,0:T(8,128)(2,1)S(1)}, u32[]{:S(2)}) copy-start(bf16[24,8,4,256]{3,1,2,0:T(8,128)(2,1)S(1)} %copy.64) | copy-start | bytes 1179652
  135.0 65.4 %all-gather.11.cloned.1.call-start = ((), (), s32[]{:S(2)}) async-start(), calls=%async_computation.9 | async-start | bytes 1769472 | tf_op jit(solution)/shard_map/all_gather | solution.py:79
  135.6 89.0 %all-gather.13.cloned.1.call-start = ((), (), s32[]{:S(2)}) async-start(), calls=%async_computation.10 | async-start | bytes 1769472 | tf_op jit(solution)/shard_map/all_gather | solution.py:80
  136.2 135.8 %all-reduce.11.cloned.1.call-start = ((), (), s32[]{:S(2)}) async-start(), calls=%async_computation.11 | async-start | bytes 3145728 | tf_op jit(solution)/shard_map/psum | solution.py:149
  176.2 2.1 copy-start.4
  179.3 157.1 %copy-start.32 = (f32[1024]{0:T(1024)}, f32[1024]{0:T(1024)S(1)}, u32[]{:S(2)}) copy-start(f32[1024]{0:T(1024)S(1)} %add_rsqrt_fusion.1) | copy-start | bytes 12292
  179.3 21.2 %copy-start.28 = (f32[768]{0:T(1024)S(1)}, f32[768]{0:T(1024)}, u32[]{:S(2)}) copy-start(f32[768]{0:T(1024)} %param.31) | copy-start | bytes 9220
  179.3 21.2 %copy-start.35 = (f32[768]{0:T(1024)S(1)}, f32[768]{0:T(1024)}, u32[]{:S(2)}) copy-start(f32[768]{0:T(1024)} %param.32) | copy-start | bytes 9220
  179.3 21.2 %copy-start.49 = (f32[768]{0:T(1024)S(1)}, f32[768]{0:T(1024)}, u32[]{:S(2)}) copy-start(f32[768]{0:T(1024)} %param.34) | copy-start | bytes 9220
  224.7 4.4 copy-start.31
  228.9 43.1 %copy-start.34 = (f32[768]{0:T(1024)S(1)}, f32[768]{0:T(1024)}, u32[]{:S(2)}) copy-start(f32[768]{0:T(1024)} %param.36) | copy-start | bytes 9220
  229.0 102.6 %all-reduce.13.cloned.1.call-start = ((), (), s32[]{:S(2)}) async-start(), calls=%async_computation.12 | async-start | bytes 3145728 | tf_op jit(solution)/shard_map/psum | solution.py:161
  272.0 2.2 copy-start.5
  277.4 2.2 copy-start.47
  277.4 3.9 copy-start.51
  279.1 5.7 copy-start.11
  281.3 4.6 copy-start.46
  285.9 45.7 %copy-start.45 = (f32[768]{0:T(1024)S(1)}, f32[768]{0:T(1024)}, u32[]{:S(2)}) copy-start(f32[768]{0:T(1024)} %param.38) | copy-start | bytes 9220
  288.5 266.1 %reduce-scatter.15.cloned.1.call-start = ((), (), s32[]{:S(2)}) async-start(), calls=%async_computation.13 | async-start | bytes 3932160 | tf_op jit(solution)/shard_map/reduce_scatter | solution.py:216
  348.2 1.9 copy-start.23
  348.2 1.9 copy-start.25
  348.2 1.9 copy-start.27
  398.3 1.9 copy-start.23
  398.3 1.9 copy-start.25
  398.3 1.9 copy-start.27
  448.3 1.9 copy-start.23
  448.3 1.9 copy-start.25
  448.3 1.9 copy-start.27
  494.0 96.6 %reduce-scatter.23.cloned.1.call-start = ((), (), s32[]{:S(2)}) async-start(), calls=%async_computation.19 | async-start | bytes 589824
  499.4 95.0 %reduce-scatter.25.cloned.1.call-start = ((), (), s32[]{:S(2)}) async-start(), calls=%async_computation.20 | async-start | bytes 1769472
  506.9 105.3 %reduce-scatter.21.cloned.1.call-start = ((), (), s32[]{:S(2)}) async-start(), calls=%async_computation.18 | async-start | bytes 884736
  559.7 9.4 %copy-start.29 = (f32[768]{0:T(1024)S(1)}, f32[768]{0:T(1024)}, u32[]{:S(2)}) copy-start(f32[768]{0:T(1024)} %param.31) | copy-start | bytes 9220
  559.7 9.4 %copy-start.36 = (f32[768]{0:T(1024)S(1)}, f32[768]{0:T(1024)}, u32[]{:S(2)}) copy-start(f32[768]{0:T(1024)} %param.32) | copy-start | bytes 9220
  569.0 67.7 %reduce-scatter.17.cloned.1.call-start = ((), (), s32[]{:S(2)}) async-start(), calls=%async_computation.16 | async-start | bytes 1769472 | tf_op jit(solution)/shard_map/reduce_scatter | solution.py:298
  573.0 5.7 copy-start.44
  573.0 155.3 %all-gather.15.cloned.1.call-start = ((), (), s32[]{:S(2)}) async-start(), calls=%async_computation.15 | async-start | bytes 5898240 | tf_op jit(solution)/shard_map/all_gather | solution.py:277
  579.9 5.0 copy-start.14
  584.8 214.1 %all-reduce.15.cloned.1.call-start = ((), (), s32[]{:S(2)}) async-start(), calls=%async_computation.14 | async-start | bytes 3145728 | tf_op jit(solution)/shard_map/psum | solution.py:243
  584.9 3.2 copy-start.10
  584.9 3.2 copy-start.13
  590.4 256.4 %all-reduce.17.cloned.1.call-start = ((), (), s32[]{:S(2)}) async-start(), calls=%async_computation.21 | async-start | bytes 3244032 | tf_op jit(solution)/shard_map/psum | solution.py:283
  636.7 233.5 %reduce-scatter.19.cloned.1.call-start = ((), (), s32[]{:S(2)}) async-start(), calls=%async_computation.17 | async-start | bytes 1769472
  740.3 7.7 copy-start.15
  743.7 55.2 %copy-start.33 = (f32[1024]{0:T(1024)S(1)}, f32[1024]{0:T(1024)}, u32[]{:S(2)}) copy-start(f32[1024]{0:T(1024)} %copy-done.32) | copy-start | bytes 12292
  743.7 55.2 %copy-start.38 = (f32[1024]{0:T(1024)S(1)}, f32[1024]{0:T(1024)}, u32[]{:S(2)}) copy-start(f32[1024]{0:T(1024)} %copy-done.37) | copy-start | bytes 12292
  743.7 55.2 %copy-start.40 = (f32[1024]{0:T(1024)S(1)}, f32[1024]{0:T(1024)}, u32[]{:S(2)}) copy-start(f32[1024]{0:T(1024)} %copy-done.39) | copy-start | bytes 12292
  846.7 5.7 copy-start.20
  (16 other events, 22.6 us)
Sparse Core Ops, SparseCore 0:
  9.5 25.4 all-gather.6
  37.2 63.4 all-gather.8
  135.2 41.0 all-reduce.8
  177.6 22.7 all-gather.10
  201.9 22.7 all-gather.12
  229.1 42.8 all-reduce.10
  288.6 42.8 all-reduce.12
  494.1 60.4 reduce-scatter.14
  556.8 13.1 reduce-scatter.22
  572.6 21.8 reduce-scatter.24
  596.7 15.3 reduce-scatter.20
  614.8 21.8 reduce-scatter.16
  638.8 89.3 all-gather.14
  730.5 41.9 all-reduce.14
  775.6 71.0 all-reduce.16
  849.4 20.8 reduce-scatter.18
